TPU v7x, 32 devices: a whole 2x2x4 slice. The times are simulated.
32 devices in a mesh: dp: 16 (over z, y, core), tensor: 2 (over x).
Axes of the slice: x: 2, y: 2, z: 4, core: 2. Of those that a mesh axis runs over, the one named last changes fastest.
Arguments:
- inputs: bfloat16 [8192, 1024], P('dp'), may hold values from -6 to 6
- first_values: bfloat16 [8192, 1024], P('dp', 'tensor'), may hold values from -6 to 6
- w_query: bfloat16 [1024, 1024], P(None, 'tensor'), may hold values from -0.1875 to 0.1875
- w_key: bfloat16 [1024, 1024], P(None, 'tensor'), may hold values from -0.1875 to 0.1875
- w_value: bfloat16 [1024, 1024], P(None, 'tensor'), may hold values from -0.1875 to 0.1875
- w_out: bfloat16 [1024, 1024], P('tensor'), may hold values from -4 to 4
- w_gate: bfloat16 [1024, 2816], P(None, 'tensor'), may hold values from -0.1875 to 0.1875
- w_up: bfloat16 [1024, 2816], P(None, 'tensor'), may hold values from -0.1875 to 0.1875
- w_down: bfloat16 [2816, 1024], P('tensor'), may hold values from -0.109375 to 0.109375
- norm_attn: bfloat16 [1024], replicated, may hold values from 0.5 to 1.5
- norm_ffn: bfloat16 [1024], replicated, may hold values from 0.5 to 1.5
- cotangent: bfloat16 [8192, 1024], P('dp'), may hold values from -6 to 6
- parents: int32 [16], replicated, may hold values from -1 to 7, as said below
- depth_pos: int32 [16], replicated, may hold values from 0 to 2560, as said below
- assignment: int32 [16], replicated, may hold values from 0 to 15, as said below
Outputs:
- output: bfloat16 [8192, 1024], P('dp')
- grad_inputs: float32 [8192, 1024], P('dp')
- grad_first_values: float32 [8192, 1024], P('dp', 'tensor')
- grad_w_query: float32 [1024, 1024], P(None, 'tensor')
- grad_w_key: float32 [1024, 1024], P(None, 'tensor')
- grad_w_value: float32 [1024, 1024], P(None, 'tensor')
- grad_w_out: float32 [1024, 1024], P('tensor')
- grad_w_gate: float32 [1024, 2816], P(None, 'tensor')
- grad_w_up: float32 [1024, 2816], P(None, 'tensor')
- grad_w_down: float32 [2816, 1024], P('tensor')
- grad_norm_attn: float32 [1024], replicated
- grad_norm_ffn: float32 [1024], replicated
Inputs may be any that keep to these rules, and one draw needn't show every extreme that they name: `parents`: the tree-ordered segments form 1 trees of 16: segment 16 k is a root, 16 k + j has parent 16 k + j - 1 for j = 1, 2, 3, segments 16 k + 4 to 16 k + 7 have parent 16 k + 3, and each of 16 k + 8 to 16 k + 15 has one of 16 k + 4 to 16 k + 7 as parent, each of those the parent of exactly two. A permutation: tree-ordered segment g lies in slot assignment[g], that is in rows assignment[g] * 512 to assignment[g] * 512 + 511. depth_pos[s] is 512 times the number of strict ancestors of the segment in slot s.
All inputs are finite; a program needn't handle non-finite values.
Results may differ from a plain program's by a relative error of at most 0.025.
Values may be sent and summed in bfloat16 or wider, within the bound.
No kernel may reach another device: no remote copies, remote signals or barrier semaphores. Data moves between devices by JAX's collectives and lax.ppermute only.
A program may use at most 256 MiB of HBM per device.

v0:
```python
import jax
import jax.numpy as jnp
from jax import lax
from jax.sharding import PartitionSpec as P

HEAD_DIM = 64
SEG = 512
epsilon = 1e-06
rope_base = 10000.0
climb_steps = 5
masked_score = -1e30


def rms_scale(values):
    return lax.rsqrt(jnp.mean(values * values, axis=-1, keepdims=True) + epsilon)


def rotary_tables(positions, head_dim):
    half_dim = head_dim // 2
    frequency = rope_base ** (-jnp.arange(half_dim, dtype=jnp.float32) * 2.0 / head_dim)
    angles = positions.astype(jnp.float32)[:, None] * frequency[None, :]
    return (jnp.cos(angles)[:, None, :], jnp.sin(angles)[:, None, :])


def rotate(values, cosine, sine_table):
    half_dim = values.shape[-1] // 2
    first_half = values[..., :half_dim]
    second_half = values[..., half_dim:]
    return jnp.concatenate(
        [
            first_half * cosine - second_half * sine_table,
            second_half * cosine + first_half * sine_table,
        ],
        axis=-1,
    )


def rotate_back(gradient, cosine, sine_table):
    half_dim = gradient.shape[-1] // 2
    first_half = gradient[..., :half_dim]
    second_half = gradient[..., half_dim:]
    return jnp.concatenate(
        [
            first_half * cosine + second_half * sine_table,
            second_half * cosine - first_half * sine_table,
        ],
        axis=-1,
    )


def parent_slots(parents, assignment):
    count = parents.shape[0]
    slot_ids = jnp.arange(count, dtype=jnp.int32)
    at_slot = assignment[None, :] == slot_ids[:, None]
    parent_seg = jnp.sum(jnp.where(at_slot, parents[None, :], 0), axis=1)
    parent_match = slot_ids[None, :] == parent_seg[:, None]
    above_slot = jnp.sum(jnp.where(parent_match, assignment[None, :], 0), axis=1)
    return jnp.where(parent_seg >= 0, above_slot, -1)


def climb(parent_slot, start_slots):
    slot_ids = jnp.arange(parent_slot.shape[0], dtype=jnp.int32)
    levels = [start_slots]
    current = start_slots
    for step_index in range(climb_steps):
        matched = current[:, None] == slot_ids[None, :]
        upward = jnp.sum(jnp.where(matched, parent_slot[None, :], 0), axis=1)
        current = jnp.where(current >= 0, upward, -1)
        levels.append(current)
    return jnp.stack(levels, axis=1)


def norm_back(grad_normed, values, row_scale, gain_vector):
    scaled_grad = grad_normed * gain_vector
    grad_gain = jnp.sum(grad_normed * values * row_scale, axis=0)
    grad_values = row_scale * (
        scaled_grad
        - values * row_scale * row_scale * jnp.mean(scaled_grad * values, axis=-1, keepdims=True)
    )
    return (grad_values, grad_gain)


def path_rows(source, path_row):
    parts = []
    for level_index in range(climb_steps + 1):
        row_begin = (jnp.maximum(path_row[level_index], 0) * SEG).astype(jnp.int32)
        parts.append(lax.dynamic_slice_in_dim(source, row_begin, SEG, 0))
    return jnp.concatenate(parts, axis=0)


def path_permit(path_row, causal):
    parts = [causal]
    for level_index in range(1, climb_steps + 1):
        parts.append(jnp.broadcast_to(path_row[level_index] >= 0, (SEG, SEG)))
    return jnp.concatenate(parts, axis=1)


def body(
    inputs,
    first_values,
    w_query,
    w_key,
    w_value,
    w_out,
    w_gate,
    w_up,
    w_down,
    norm_attn,
    norm_ffn,
    cotangent,
    parents,
    depth_pos,
    assignment,
):
    row_count = inputs.shape[0]
    local_width = w_query.shape[1]
    head_count = local_width // HEAD_DIM
    score_scale = HEAD_DIM ** (-0.5)
    seg_count = row_count // SEG
    slot_total = parents.shape[0]
    slot_ids = jnp.arange(slot_total, dtype=jnp.int32)
    local_rows = jnp.arange(row_count, dtype=jnp.int32)
    own_slots = lax.axis_index("dp") * seg_count + jnp.arange(seg_count, dtype=jnp.int32)
    own_slot_rows = jnp.repeat(own_slots, SEG)
    depth_rows = jnp.sum(
        jnp.where(own_slot_rows[:, None] == slot_ids[None, :], depth_pos[None, :], 0), axis=1
    )
    positions = depth_rows + local_rows % SEG
    parent_slot = parent_slots(parents, assignment)
    own_paths = climb(parent_slot, own_slots)
    offsets = jnp.arange(SEG, dtype=jnp.int32)
    causal = offsets[None, :] <= offsets[:, None]
    cosine, sine_table = rotary_tables(positions, HEAD_DIM)
    inputs_wide = inputs.astype(jnp.float32)
    attn_scale = rms_scale(inputs_wide)
    gain_attn = norm_attn.astype(jnp.float32)
    normed = (inputs_wide * attn_scale * gain_attn).astype(jnp.bfloat16)
    query_proj = jnp.dot(normed, w_query, preferred_element_type=jnp.float32)
    key_proj = jnp.dot(normed, w_key, preferred_element_type=jnp.float32)
    value_proj = jnp.dot(normed, w_value, preferred_element_type=jnp.float32)
    query_rot = rotate(
        query_proj.reshape(row_count, head_count, HEAD_DIM), cosine, sine_table
    ).astype(jnp.bfloat16)
    key_rot = (
        rotate(key_proj.reshape(row_count, head_count, HEAD_DIM), cosine, sine_table)
        .astype(jnp.bfloat16)
        .reshape(row_count, local_width)
    )
    mixed = (0.5 * value_proj + 0.5 * first_values.astype(jnp.float32)).astype(jnp.bfloat16)
    key_all, value_all = (
        lax.all_gather(key_rot, "dp", axis=0, tiled=True),
        lax.all_gather(mixed, "dp", axis=0, tiled=True),
    )
    query_segs = query_rot.reshape(seg_count, SEG, head_count, HEAD_DIM)

    def segment_forward(operand):
        query_block, path_row = operand
        near_keys = path_rows(key_all, path_row).reshape(-1, head_count, HEAD_DIM)
        near_values = path_rows(value_all, path_row).reshape(-1, head_count, HEAD_DIM)
        permit = path_permit(path_row, causal)
        scores = (
            jnp.einsum("qhd,khd->hqk", query_block, near_keys, preferred_element_type=jnp.float32)
            * score_scale
        )
        scores = jnp.where(permit[None], scores, masked_score)
        row_max = jnp.max(scores, axis=-1)
        weights = jnp.where(permit[None], jnp.exp(scores - row_max[..., None]), 0.0)
        row_total = jnp.sum(weights, axis=-1)
        attn_probs = weights / row_total[..., None]
        block_out = jnp.einsum(
            "hqk,khd->qhd",
            attn_probs.astype(jnp.bfloat16),
            near_values,
            preferred_element_type=jnp.float32,
        )
        return (block_out, row_max + jnp.log(row_total))

    attn_parts, log_parts = lax.map(segment_forward, (query_segs, own_paths))
    attn_exact = attn_parts.reshape(row_count, head_count, HEAD_DIM)
    attended = attn_exact.reshape(row_count, local_width).astype(jnp.bfloat16)
    branch_attn = lax.psum(
        jnp.dot(attended, w_out, preferred_element_type=jnp.float32).astype(jnp.bfloat16), "tensor"
    ).astype(jnp.float32)
    hidden_state = inputs_wide + branch_attn
    ffn_scale = rms_scale(hidden_state)
    gain_ffn = norm_ffn.astype(jnp.float32)
    normed_ffn = (hidden_state * ffn_scale * gain_ffn).astype(jnp.bfloat16)
    gate_proj = jnp.dot(normed_ffn, w_gate, preferred_element_type=jnp.float32)
    up_proj = jnp.dot(normed_ffn, w_up, preferred_element_type=jnp.float32)
    silu_gate = jax.nn.silu(gate_proj)
    activated = (silu_gate * up_proj).astype(jnp.bfloat16)
    feed = lax.psum(
        jnp.dot(activated, w_down, preferred_element_type=jnp.float32).astype(jnp.bfloat16),
        "tensor",
    ).astype(jnp.float32)
    output = (hidden_state + feed).astype(jnp.bfloat16)
    grad_w_down = jnp.einsum("tf,td->fd", activated, cotangent, preferred_element_type=jnp.float32)
    grad_activated = jnp.einsum("td,fd->tf", cotangent, w_down, preferred_element_type=jnp.float32)
    sigmoid_gate = jax.nn.sigmoid(gate_proj)
    grad_gate = (
        grad_activated * up_proj * sigmoid_gate * (1.0 + gate_proj * (1.0 - sigmoid_gate))
    ).astype(jnp.bfloat16)
    grad_up = (grad_activated * silu_gate).astype(jnp.bfloat16)
    grad_w_gate = jnp.einsum("td,tf->df", normed_ffn, grad_gate, preferred_element_type=jnp.float32)
    grad_w_up = jnp.einsum("td,tf->df", normed_ffn, grad_up, preferred_element_type=jnp.float32)
    ffn_partial = jnp.einsum(
        "tf,df->td", grad_gate, w_gate, preferred_element_type=jnp.float32
    ) + jnp.einsum("tf,df->td", grad_up, w_up, preferred_element_type=jnp.float32)
    grad_normed_ffn = lax.psum(ffn_partial.astype(jnp.bfloat16), "tensor").astype(jnp.float32)
    grad_hidden_norm, grad_gain_ffn = norm_back(grad_normed_ffn, hidden_state, ffn_scale, gain_ffn)
    grad_hidden = cotangent.astype(jnp.float32) + grad_hidden_norm
    grad_branch = grad_hidden.astype(jnp.bfloat16)
    grad_w_out = jnp.einsum("tc,td->cd", attended, grad_branch, preferred_element_type=jnp.float32)
    grad_attended = jnp.einsum(
        "td,cd->tc", grad_branch, w_out, preferred_element_type=jnp.float32
    ).astype(jnp.bfloat16)
    grad_heads = grad_attended.reshape(row_count, head_count, HEAD_DIM)
    delta_rows = jnp.sum(grad_heads.astype(jnp.float32) * attn_exact, axis=-1)
    delta_parts = jnp.transpose(delta_rows.reshape(seg_count, SEG, head_count), (0, 2, 1))
    grad_segs = grad_heads.reshape(seg_count, SEG, head_count, HEAD_DIM)
    key_back, value_back = (key_all, value_all)

    def segment_back(query_block, grad_block, path_row, log_block, delta_block):
        near_keys = path_rows(key_back, path_row).reshape(-1, head_count, HEAD_DIM)
        near_values = path_rows(value_back, path_row).reshape(-1, head_count, HEAD_DIM)
        permit = path_permit(path_row, causal)
        scores = (
            jnp.einsum("qhd,khd->hqk", query_block, near_keys, preferred_element_type=jnp.float32)
            * score_scale
        )
        scores = jnp.where(permit[None], scores, masked_score)
        attn_probs = jnp.where(permit[None], jnp.exp(scores - log_block[..., None]), 0.0)
        grad_probs = jnp.einsum(
            "qhd,khd->hqk", grad_block, near_values, preferred_element_type=jnp.float32
        )
        grad_scores = (attn_probs * (grad_probs - delta_block[..., None])).astype(jnp.bfloat16)
        grad_part = (
            jnp.einsum("hqk,khd->qhd", grad_scores, near_keys, preferred_element_type=jnp.float32)
            * score_scale
        )
        return (attn_probs, grad_scores, grad_part)

    zero_rows = jnp.zeros((key_back.shape[0], local_width), jnp.float32)

    def scatter_step(fold_state, operand):
        key_acc, value_acc = fold_state
        query_block, grad_block, path_row, log_block, delta_block = operand
        attn_probs, grad_scores, grad_part = segment_back(
            query_block, grad_block, path_row, log_block, delta_block
        )
        key_term = (
            jnp.einsum("hqk,qhd->khd", grad_scores, query_block, preferred_element_type=jnp.float32)
            * score_scale
        ).reshape(climb_steps + 1, SEG, local_width)
        value_term = jnp.einsum(
            "hqk,qhd->khd",
            attn_probs.astype(jnp.bfloat16),
            grad_block,
            preferred_element_type=jnp.float32,
        ).reshape(climb_steps + 1, SEG, local_width)
        for level_index in range(climb_steps + 1):
            row_begin = (jnp.maximum(path_row[level_index], 0) * SEG).astype(jnp.int32)
            key_acc = lax.dynamic_update_slice_in_dim(
                key_acc,
                lax.dynamic_slice_in_dim(key_acc, row_begin, SEG, 0) + key_term[level_index],
                row_begin,
                0,
            )
            value_acc = lax.dynamic_update_slice_in_dim(
                value_acc,
                lax.dynamic_slice_in_dim(value_acc, row_begin, SEG, 0) + value_term[level_index],
                row_begin,
                0,
            )
        return ((key_acc, value_acc), grad_part)

    (key_terms, value_terms), grad_parts = lax.scan(
        scatter_step,
        (zero_rows, zero_rows),
        (query_segs, grad_segs, own_paths, log_parts, delta_parts),
    )
    grad_query_rot = grad_parts.reshape(row_count, head_count, HEAD_DIM)
    key_sums, value_sums = (
        lax.psum_scatter(
            key_terms.astype(jnp.bfloat16), "dp", scatter_dimension=0, tiled=True
        ).astype(jnp.float32),
        lax.psum_scatter(
            value_terms.astype(jnp.bfloat16), "dp", scatter_dimension=0, tiled=True
        ).astype(jnp.float32),
    )
    grad_key_rot = key_sums.reshape(row_count, head_count, HEAD_DIM)
    grad_first_values = 0.5 * value_sums
    grad_value = (0.5 * value_sums).astype(jnp.bfloat16)
    grad_key = (
        rotate_back(grad_key_rot, cosine, sine_table)
        .reshape(row_count, local_width)
        .astype(jnp.bfloat16)
    )
    grad_query = (
        rotate_back(grad_query_rot, cosine, sine_table)
        .reshape(row_count, local_width)
        .astype(jnp.bfloat16)
    )
    grad_w_query = jnp.einsum("td,tc->dc", normed, grad_query, preferred_element_type=jnp.float32)
    grad_w_key = jnp.einsum("td,tc->dc", normed, grad_key, preferred_element_type=jnp.float32)
    grad_w_value = jnp.einsum("td,tc->dc", normed, grad_value, preferred_element_type=jnp.float32)
    attn_partial = (
        jnp.einsum("tc,dc->td", grad_query, w_query, preferred_element_type=jnp.float32)
        + jnp.einsum("tc,dc->td", grad_key, w_key, preferred_element_type=jnp.float32)
        + jnp.einsum("tc,dc->td", grad_value, w_value, preferred_element_type=jnp.float32)
    )
    grad_normed = lax.psum(attn_partial.astype(jnp.bfloat16), "tensor").astype(jnp.float32)
    grad_input_norm, grad_gain_attn = norm_back(grad_normed, inputs_wide, attn_scale, gain_attn)
    grad_inputs = grad_hidden + grad_input_norm
    summed = (
        lax.psum(grad_w_query.astype(jnp.bfloat16), "dp").astype(jnp.float32),
        lax.psum(grad_w_key.astype(jnp.bfloat16), "dp").astype(jnp.float32),
        lax.psum(grad_w_value.astype(jnp.bfloat16), "dp").astype(jnp.float32),
        lax.psum(grad_w_out.astype(jnp.bfloat16), "dp").astype(jnp.float32),
        lax.psum(grad_w_gate.astype(jnp.bfloat16), "dp").astype(jnp.float32),
        lax.psum(grad_w_up.astype(jnp.bfloat16), "dp").astype(jnp.float32),
        lax.psum(grad_w_down.astype(jnp.bfloat16), "dp").astype(jnp.float32),
        lax.psum(grad_gain_attn.astype(jnp.bfloat16), "dp").astype(jnp.float32),
        lax.psum(grad_gain_ffn.astype(jnp.bfloat16), "dp").astype(jnp.float32),
    )
    return (
        output,
        grad_inputs,
        grad_first_values,
        summed[0],
        summed[1],
        summed[2],
        summed[3],
        summed[4],
        summed[5],
        summed[6],
        summed[7],
        summed[8],
    )


def solution(mesh):
    placed = (
        P("dp", None),
        P("dp", "tensor"),
        P(None, "tensor"),
        P(None, "tensor"),
        P(None, "tensor"),
        P("tensor", None),
        P(None, "tensor"),
        P(None, "tensor"),
        P("tensor", None),
        P(),
        P(),
        P("dp", None),
        P(),
        P(),
        P(),
    )
    return jax.shard_map(
        body,
        mesh=mesh,
        in_specs=placed,
        out_specs=(
            P("dp", None),
            P("dp", None),
            P("dp", "tensor"),
            P(None, "tensor"),
            P(None, "tensor"),
            P(None, "tensor"),
            P("tensor", None),
            P(None, "tensor"),
            P(None, "tensor"),
            P("tensor", None),
            P(),
            P(),
        ),
        check_vma=False,
    )
```

profile of v0, /device:TPU:0, one launch (start us, length us, event | category | flops | bytes accessed | tf_op | source)
XLA Modules:
  0.0 1030.7 jit_solution(15380133713444836444)
XLA Ops:
  29.8 60.8 %all-gather.3.cloned.1.call-done = bf16[8192,512]{1,0:T(8,128)(2,1)} async-done(((bf16[512,512]{1,0:T(8,128)(2,1)}), bf16[8192,512]{1,0:T(8,128)(2,1)}) %all-gather.3.cloned.1.call-update) | async-done | bytes 8388624 | tf_op jit(solution)/shard_map/all_gather | solution.py:152
  101.9 4.8 copy.57
  106.7 63.1 %all-gather.5.cloned.1.call-done = bf16[8192,512]{0,1:T(8,128)(2,1)} async-done(((bf16[512,512]{0,1:T(8,128)(2,1)}), bf16[8192,512]{0,1:T(8,128)(2,1)}) %all-gather.5.cloned.1.call-update) | async-done | bytes 8388624 | tf_op jit(solution)/shard_map/all_gather | solution.py:151
  180.9 22.8 %fusion.2 = (f32[8,512]{1,0:T(8,128)S(1)}, f32[8,512,3072]{2,1,0:T(8,128)}) fusion(pred[512,3072]{1,0:T(8,128)(4,1)} %broadcast_dynamic-update-slice_fusion, bf16[3072,8,64]{0,2,1:T(8,128)(2,1)} %bitcast.4, bf16[512,8,32]{0,2,1:T(8,128)(2,1)S(1)} %get-tuple-element.111, bf16[512,8,32]{0,2,1:T(8,128)(2,1)S(1)} %get-tuple-element.110), kind=kOutput, calls=%fused_computation.7 | convolution fusion | flops 1649405952 | bytes 55590912 | tf_op jit(solution)/shard_map/while/body/eval_jaxpr/qhd,khd->hqk/dot_general | solution.py:162
  203.7 23.2 %fusion = f32[8,512]{1,0:T(8,128)S(1)} fusion(f32[8,512,3072]{2,1,0:T(8,128)} %get-tuple-element.121, f32[8,512]{1,0:T(8,128)S(1)} %get-tuple-element.120, pred[512,3072]{1,0:T(8,128)(4,1)} %broadcast_dynamic-update-slice_fusion), kind=kLoop, calls=%fused_computation.5 | loop fusion | flops 62910464 | bytes 51937280 | tf_op jit(solution)/shard_map/while/body/eval_jaxpr/reduce_sum | solution.py:168
  226.9 22.0 %fusion.68 = (bf16[512,8,64]{0,2,1:T(8,128)(2,1)S(1)}, f32[512,8,64]{0,2,1:T(8,128)}) fusion(bf16[3072,8,64]{0,2,1:T(8,128)(2,1)S(1)} %bitcast.90, f32[8,512,3072]{2,1,0:T(8,128)} %get-tuple-element.121, f32[8,512]{1,0:T(8,128)S(1)} %fusion, f32[8,512]{1,0:T(8,128)S(1)} %get-tuple-element.120, pred[512,3072]{1,0:T(8,128)(4,1)} %broadcast_dynamic-update-slice_fusion), kind=kOutput, calls=%fused_computation.158 | convolution fusion | flops 1686372352 | bytes 56655872 | tf_op jit(solution)/shard_map/while/body/eval_jaxpr/hqk,khd->qhd/dot_general | solution.py:170
  251.7 38.1 %all-reduce.8.cloned.1.call-done = bf16[512,1024]{1,0:T(8,128)(2,1)} async-done(((bf16[512,1024]{1,0:T(8,128)(2,1)}), bf16[512,1024]{1,0:T(8,128)(2,1)}) %all-reduce.8.cloned.1.call-update) | async-done | bytes 1048592 | tf_op jit(solution)/shard_map/psum | solution.py:181
  306.6 40.1 %all-reduce.10.cloned.1.call-done = bf16[512,1024]{1,0:T(8,128)(2,1)} async-done(((bf16[512,1024]{1,0:T(8,128)(2,1)}), bf16[512,1024]{1,0:T(8,128)(2,1)}) %all-reduce.10.cloned.1.call-update) | async-done | bytes 1048592 | tf_op jit(solution)/shard_map/psum | solution.py:209
  354.2 24.3 %fusion.7 = f32[3072,8,64]{0,2,1:T(8,128)} fusion(bf16[512,8,64]{0,2,1:T(8,128)(2,1)} %bitcast.100, f32[8,512,3072]{2,1,0:T(8,128)} %get-tuple-element.121, f32[8,512]{1,0:T(8,128)S(1)} %log_add_fusion, pred[512,3072]{1,0:T(8,128)(4,1)} %broadcast_dynamic-update-slice_fusion), kind=kOutput, calls=%fused_computation.12 | convolution fusion | flops 1673527296 | bytes 58736640 | tf_op jit(solution)/shard_map/while/body/eval_jaxpr/hqk,qhd->khd/dot_general | solution.py:255
  378.5 32.9 %multiply_convert_fusion = bf16[8,512,3072]{2,1,0:T(8,128)(2,1)} fusion(f32[8,512,3072]{2,1,0:T(8,128)} %get-tuple-element.121, bf16[512,8,64]{0,2,1:T(8,128)(2,1)} %bitcast.101, bf16[3072,8,64]{0,2,1:T(8,128)(2,1)} %bitcast.89, f32[8,512]{1,0:T(8,128)S(1)} %bitcast.102, f32[8,512]{1,0:T(8,128)S(1)} %log_add_fusion, ...), kind=kOutput, calls=%fused_computation | convolution fusion | flops 1698693120 | bytes 80773120 | tf_op jit(solution)/shard_map/while/body/eval_jaxpr/qhd,khd->hqk/dot_general | solution.py:233
  411.4 10.7 %multiply_bitcast_fusion = f32[3072,8,64]{0,2,1:T(8,128)S(1)} fusion(bf16[8,512,3072]{2,1,0:T(8,128)(2,1)} %multiply_convert_fusion, bf16[512,8,32]{0,2,1:T(8,128)(2,1)S(1)} %copy-done.26, bf16[512,8,32]{0,2,1:T(8,128)(2,1)S(1)} %copy-done.24), kind=kOutput, calls=%fused_computation.11 | convolution fusion | flops 1613234176 | bytes 31981568 | tf_op jit(solution)/shard_map/while/body/eval_jaxpr/hqk,qhd->khd/dot_general | solution.py:252
  429.9 5.6 fusion.66
  453.1 7.9 broadcast_in_dim.186.clone
  494.0 9.2 convert_element_type.206
  507.5 14.5 %fusion.31 = f32[512,8,64]{0,2,1:T(8,128)} fusion(bf16[3072,8,64]{0,2,1:T(8,128)(2,1)} %bitcast.4, bf16[8,512,3072]{2,1,0:T(8,128)(2,1)} %multiply_convert_fusion), kind=kOutput, calls=%fused_computation.62 | convolution fusion | flops 1610874880 | bytes 29360128 | tf_op jit(solution)/shard_map/while/body/eval_jaxpr/hqk,khd->qhd/dot_general | solution.py:238
  521.9 55.6 %reduce-scatter.3.cloned.1.call-done = bf16[512,512]{1,0:T(8,128)(2,1)} async-done(((bf16[8192,512]{1,0:T(8,128)(2,1)}), bf16[512,512]{1,0:T(8,128)(2,1)}) %reduce-scatter.3.cloned.1.call-update) | async-done | bytes 524304 | tf_op jit(solution)/shard_map/reduce_scatter | solution.py:284
  586.0 99.8 %reduce-scatter.5.cloned.1.call-done = bf16[512,512]{1,0:T(8,128)(2,1)} async-done(((bf16[8192,512]{1,0:T(8,128)(2,1)}), bf16[512,512]{1,0:T(8,128)(2,1)}) %reduce-scatter.5.cloned.1.call-update) | async-done | bytes 524304 | tf_op jit(solution)/shard_map/reduce_scatter | solution.py:287
  688.0 4.3 add_convert_fusion
  692.3 5.2 convolution_convert_fusion.1
  712.4 42.9 %all-reduce.14.cloned.1.call-done = (bf16[512,1024]{1,0:T(8,128)(2,1)}, bf16[512,1024]{1,0:T(8,128)(2,1)}) async-done(((bf16[512,1024]{1,0:T(8,128)(2,1)}, bf16[512,1024]{1,0:T(8,128)(2,1)}), (bf16[512,1024]{1,0:T(8,128)(2,1)}, bf16[512,1024]{1,0:T(8,128)(2,1)})) %all-reduce.14.cloned.1.call-update) | async-done | bytes 2097168 | tf_op jit(solution)/shard_map/psum | solution.py:192
  757.7 34.7 %all-reduce = (bf16[1024]{0:T(1024)(128)(2,1)S(1)}, bf16[1024]{0:T(1024)(128)(2,1)S(1)}) all-reduce(bf16[1024]{0:T(1024)(128)(2,1)S(1)} %get-tuple-element.62, bf16[1024]{0:T(1024)(128)(2,1)S(1)} %copy-done.54), channel_id=1, replica_groups=mesh['dp'=16,'tensor'=2] {'dp'}, use_global_device_ids=true, to_apply=%region_29.30 | all-reduce | flops 2048 | bytes 8192 | tf_op jit(solution)/shard_map/psum | solution.py:323
  793.6 4.9 fusion.19
  798.5 207.5 %all-reduce.12.cloned.1.call-done = (bf16[1024,512]{1,0:T(8,128)(2,1)}, bf16[1024,512]{1,0:T(8,128)(2,1)}, bf16[1024,512]{1,0:T(8,128)(2,1)}, bf16[512,1024]{1,0...) async-done(((bf16[1024,512]{1,0:T(8,128)(2,1)}, bf16[1024,512]{1,0:T(8,128)(2,1)}, bf16[1024,512]{1,0:T(8,128)(2,1)}, ...) | async-done | bytes 12845072 | tf_op jit(solution)/shard_map/psum | solution.py:316
  1006.0 4.9 convert_element_type.220
  (254 shorter events, 172.6 us)
Async XLA Ops:
  7.2 290.7 %copy-start = (bf16[1408,1024]{1,0:T(8,128)(2,1)S(1)}, bf16[1408,1024]{1,0:T(8,128)(2,1)}, u32[]{:S(2)}) copy-start(bf16[1408,1024]{1,0:T(8,128)(2,1)} %param.23) | copy-start | bytes 8650756
  7.2 83.4 %all-gather.3.cloned.1.call-start = ((), (), s32[]{:S(2)}) async-start(), calls=%async_computation.2 | async-start | bytes 8912896 | tf_op jit(solution)/shard_map/all_gather | solution.py:152
  8.9 7.1 copy-start.50
  9.6 6.4 copy-start.46
  12.9 156.8 %all-gather.5.cloned.1.call-start = ((), (), s32[]{:S(2)}) async-start(), calls=%async_computation.3 | async-start | bytes 8912896 | tf_op jit(solution)/shard_map/all_gather | solution.py:151
  17.3 163.6 %copy-start.23 = (bf16[512,8,32]{0,2,1:T(8,128)(2,1)}, bf16[512,8,32]{0,2,1:T(8,128)(2,1)S(1)}, u32[]{:S(2)}) copy-start(bf16[512,8,32]{0,2,1:T(8,128)(2,1)S(1)} %get-tuple-element.110) | copy-start | bytes 786436
  17.3 163.6 %copy-start.25 = (bf16[512,8,32]{0,2,1:T(8,128)(2,1)}, bf16[512,8,32]{0,2,1:T(8,128)(2,1)S(1)}, u32[]{:S(2)}) copy-start(bf16[512,8,32]{0,2,1:T(8,128)(2,1)S(1)} %get-tuple-element.111) | copy-start | bytes 786436
  18.3 271.5 %all-reduce.8.cloned.1.call-start = ((), (), s32[]{:S(2)}) async-start(), calls=%async_computation.4 | async-start | bytes 2097152 | tf_op jit(solution)/shard_map/psum | solution.py:181
  203.7 23.2 %copy-start.20 = (bf16[3072,512]{0,1:T(8,128)(2,1)S(1)}, bf16[3072,512]{0,1:T(8,128)(2,1)}, u32[]{:S(2)}) copy-start(bf16[3072,512]{0,1:T(8,128)(2,1)} %copy.57) | copy-start | bytes 9437188
  226.9 22.8 %copy-start.59 = (bf16[512,1024]{1,0:T(8,128)(2,1)S(1)}, bf16[512,1024]{1,0:T(8,128)(2,1)}, u32[]{:S(2)}) copy-start(bf16[512,1024]{1,0:T(8,128)(2,1)} %param.20) | copy-start | bytes 3145732
  251.4 95.3 %all-reduce.10.cloned.1.call-start = ((), (), s32[]{:S(2)}) async-start(), calls=%async_computation.5 | async-start | bytes 2097152 | tf_op jit(solution)/shard_map/psum | solution.py:209
  251.7 98.5 %copy-start.44 = (f32[1024]{0:T(1024)}, f32[1024]{0:T(1024)S(1)}, u32[]{:S(2)}) copy-start(f32[1024]{0:T(1024)S(1)} %convert_element_type.187) | copy-start | bytes 12292
  291.9 58.3 %copy-start.48 = (f32[512]{0:T(512)}, f32[512]{0:T(512)S(1)}, u32[]{:S(2)}) copy-start(f32[512]{0:T(512)S(1)} %add_rsqrt_fusion) | copy-start | bytes 6148
  306.5 271.0 %reduce-scatter.3.cloned.1.call-start = ((), (), s32[]{:S(2)}) async-start(), calls=%async_computation.6 | async-start | bytes 8912896 | tf_op jit(solution)/shard_map/reduce_scatter | solution.py:284
  378.5 32.9 %copy-start.24 = (bf16[512,8,32]{0,2,1:T(8,128)(2,1)S(1)}, bf16[512,8,32]{0,2,1:T(8,128)(2,1)}, u32[]{:S(2)}) copy-start(bf16[512,8,32]{0,2,1:T(8,128)(2,1)} %copy-done.23) | copy-start | bytes 786436
  378.5 32.9 %copy-start.26 = (bf16[512,8,32]{0,2,1:T(8,128)(2,1)S(1)}, bf16[512,8,32]{0,2,1:T(8,128)(2,1)}, u32[]{:S(2)}) copy-start(bf16[512,8,32]{0,2,1:T(8,128)(2,1)} %copy-done.25) | copy-start | bytes 786436
  453.0 10.2 copy-start.8
  453.1 10.2 copy-start.9
  472.8 213.1 %reduce-scatter.5.cloned.1.call-start = ((), (), s32[]{:S(2)}) async-start(), calls=%async_computation.7 | async-start | bytes 8912896 | tf_op jit(solution)/shard_map/reduce_scatter | solution.py:287
  503.2 252.1 %all-reduce.14.cloned.1.call-start = ((), (), s32[]{:S(2)}) async-start(), calls=%async_computation.9 | async-start | bytes 4194304 | tf_op jit(solution)/shard_map/psum | solution.py:192
  507.4 72.3 %copy-start.41 = (f32[512,32]{0,1:T(8,128)S(1)}, f32[512,32]{0,1:T(8,128)}, u32[]{:S(2)}) copy-start(f32[512,32]{0,1:T(8,128)} %copy-done.40) | copy-start | bytes 196612
  507.4 72.3 %copy-start.43 = (f32[512,32]{0,1:T(8,128)S(1)}, f32[512,32]{0,1:T(8,128)}, u32[]{:S(2)}) copy-start(f32[512,32]{0,1:T(8,128)} %copy-done.42) | copy-start | bytes 196612
  692.3 313.7 %all-reduce.12.cloned.1.call-start = ((), (), s32[]{:S(2)}) async-start(), calls=%async_computation.8 | async-start | bytes 25690112 | tf_op jit(solution)/shard_map/psum | solution.py:316
  712.3 45.4 %copy-start.54 = (bf16[1024]{0:T(1024)(128)(2,1)S(1)}, bf16[1024]{0:T(1024)(128)(2,1)}, u32[]{:S(2)}) copy-start(bf16[1024]{0:T(1024)(128)(2,1)} %get-tuple-element.60) | copy-start | bytes 6148
  (52 other events, 152.3 us)
Sparse Core Ops, SparseCore 0:
  13.0 77.5 all-gather.2
  93.3 76.3 all-gather.4
  251.5 38.2 all-reduce.7
  306.6 40.0 all-reduce.9
  472.9 104.6 reduce-scatter.2
  581.4 104.3 reduce-scatter.4
  692.4 62.8 all-reduce.13
  762.9 243.0 all-reduce.11
where the time goes:
time: 1040 us; the launch traced here: 1030 us
  waiting for transfers between devices  608 us (58%)
  matrix products  184 us (18%)
  other arithmetic  95.9 us (9%)
  local copies, waits for them, and re-layouts  89 us (9%)
  blocking collectives  34.7 us (3%)
  between operations  18.5 us (2%)
    psum x1, waiting for transfers between devices, body(): lax.psum(grad_w_query.astype(jnp.bfloat16), 'dp').astype(jnp.float32)  207 us
    reduce_scatter x1, waiting for transfers between devices, body(): lax.psum_scatter(value_terms.astype(jnp.bfloat16), 'dp', scatter_dimensio...  99.8 us
    all_gather x1, waiting for transfers between devices, body(): lax.all_gather(key_rot, 'dp', axis=0, tiled=True)  63.1 us
    all_gather x1, waiting for transfers between devices, body(): lax.all_gather(mixed, 'dp', axis=0, tiled=True)  60.8 us
    reduce_scatter x1, waiting for transfers between devices, body(): lax.psum_scatter(key_terms.astype(jnp.bfloat16), 'dp', scatter_dimension=...  55.6 us
    psum x1, waiting for transfers between devices, body(): lax.psum(jnp.dot(activated, w_down, preferred_element_type=jnp.float32).a...  42.9 us
    psum x1, waiting for transfers between devices, body(): lax.psum(ffn_partial.astype(jnp.bfloat16), 'tensor').astype(jnp.float32)  40.1 us
    psum x1, waiting for transfers between devices, body(): lax.psum(jnp.dot(attended, w_out, preferred_element_type=jnp.float32).ast...  38.1 us
  transfers between devices with their start and end apart: 8, of which 8 were waited for; matrix products, arithmetic and copies ran while one was open for 11% of the time, Pallas kernels for 0%

commit v1 on v0

--- a/solution.py
+++ b/solution.py
@@ -9,6 +9,28 @@
 rope_base = 10000.0
 climb_steps = 5
 masked_score = -1e30
+
+
+def laid_out(blocks, dim):
+    lengths = list(blocks.shape[1:])
+    lengths[dim] *= blocks.shape[0]
+    return jnp.moveaxis(blocks, 0, dim).reshape(lengths)
+
+
+def grow_blocks(x, axis):
+    count = lax.axis_size(axis)
+    pieces = x[None]
+    for level in range(count.bit_length() - 1):
+        distance = 1 << level
+        partner_block = lax.ppermute(pieces, axis, [(i, i ^ distance) for i in range(count)])
+        both = jnp.stack([pieces, partner_block])
+        upper = lax.axis_index(axis) >> level & 1
+        pieces = jnp.where(upper == 0, both, both[::-1]).reshape(-1, *x.shape)
+    return pieces
+
+
+def gather_by_bits(x, axis, dim):
+    return laid_out(grow_blocks(x, axis), dim)
 
 
 def rms_scale(values):
@@ -149,7 +171,7 @@
     mixed = (0.5 * value_proj + 0.5 * first_values.astype(jnp.float32)).astype(jnp.bfloat16)
     key_all, value_all = (
         lax.all_gather(key_rot, "dp", axis=0, tiled=True),
-        lax.all_gather(mixed, "dp", axis=0, tiled=True),
+        gather_by_bits(mixed, "dp", 0),
     )
     query_segs = query_rot.reshape(seg_count, SEG, head_count, HEAD_DIM)
 

time: 1040 us -> 1260 us (1.21)
  waiting for transfers between devices: 608 us -> 778 us
  other arithmetic: 95.9 us -> 130 us
    ppermute x0 -> x4, waiting for transfers between devices: none -> 279 us  [grow_blocks(): lax.ppermute(pieces, axis, [(i, i ^ distance) for i in range(count)])]
    all_gather x1, waiting for transfers between devices: 63.1 us -> 0.01 us  [body(): lax.all_gather(key_rot, 'dp', axis=0, tiled=True)]
    all_gather x1 -> x0, waiting for transfers between devices: 60.8 us -> none  [body(): lax.all_gather(mixed, 'dp', axis=0, tiled=True)]
    select_n x0 -> x3, other arithmetic: none -> 16.4 us  [grow_blocks(): pieces = jnp.where(upper == 0, both, both[::-1]).reshape(-1, *x.shape)]
    another operation x2 -> x7, other arithmetic: 2.29 us -> 18.5 us  [the longest x5 14.7 us: grow_blocks(): both = jnp.stack([pieces, partner_block])]
    reduce_scatter x1, waiting for transfers between devices: 55.6 us -> 69.2 us  [body(): lax.psum_scatter(key_terms.astype(jnp.bfloat16), 'dp', scatter_dimension=...]
    unnamed x150 -> x162, local copies, waits for them, and re-layouts: 26 us -> 35.5 us
  transfers between devices with their start and end apart: 8 -> 11, of which waited for: 8 -> 10; matrix products, arithmetic and copies ran while one was open for 11% -> 11% of each run, Pallas kernels for 0% -> 0%
where the time goes in v1:
time: 1260 us; the launch traced here: 1250 us
  waiting for transfers between devices  778 us (62%)
  matrix products  187 us (15%)
  other arithmetic  130 us (10%)
  local copies, waits for them, and re-layouts  94.8 us (8%)
  blocking collectives  34.7 us (3%)
  between operations  18.4 us (1%)
    ppermute x4, waiting for transfers between devices, grow_blocks(): lax.ppermute(pieces, axis, [(i, i ^ distance) for i in range(count)])  279 us
    psum x1, waiting for transfers between devices, body(): lax.psum(grad_w_query.astype(jnp.bfloat16), 'dp').astype(jnp.float32)  207 us
    reduce_scatter x1, waiting for transfers between devices, body(): lax.psum_scatter(value_terms.astype(jnp.bfloat16), 'dp', scatter_dimensio...  99.8 us
    reduce_scatter x1, waiting for transfers between devices, body(): lax.psum_scatter(key_terms.astype(jnp.bfloat16), 'dp', scatter_dimension=...  69.2 us
    psum x1, waiting for transfers between devices, body(): lax.psum(jnp.dot(activated, w_down, preferred_element_type=jnp.float32).a...  42.9 us
    psum x1, waiting for transfers between devices, body(): lax.psum(ffn_partial.astype(jnp.bfloat16), 'tensor').astype(jnp.float32)  40.1 us
    psum x1, waiting for transfers between devices, body(): lax.psum(jnp.dot(attended, w_out, preferred_element_type=jnp.float32).ast...  40.1 us
    unnamed x162, local copies, waits for them, and re-layouts  35.5 us
  transfers between devices with their start and end apart: 11, of which 10 were waited for; matrix products, arithmetic and copies ran while one was open for 11% of the time, Pallas kernels for 0%

profile of v1, /device:TPU:0, one launch (start us, length us, event | category | flops | bytes accessed | tf_op | source)
XLA Modules:
  0.0 1251.8 jit_solution(12057462478106885250)
XLA Ops:
  30.1 29.4 %collective-permute-done.1 = bf16[2,512,512]{2,1,0:T(8,128)(2,1)} collective-permute-done((bf16[2,512,512]{2,1,0:T(8,128)(2,1)}, bf16[2,512,512]{2,1,0:T(8,128)(2,1)}, u32[]{:S(2)}, u32[]{:S(2)}) %collective-permute-start.1) | collective-permute-done | bytes 1048608 | tf_op jit(solution)/shard_map/ppermute | solution.py:25
  64.8 78.1 %collective-permute-done.2 = bf16[4,512,512]{2,1,0:T(8,128)(2,1)} collective-permute-done((bf16[4,512,512]{2,1,0:T(8,128)(2,1)}, bf16[4,512,512]{2,1,0:T(8,128)(2,1)}, u32[]{:S(2)}, u32[]{:S(2)}) %collective-permute-start.2) | collective-permute-done | bytes 2097184 | tf_op jit(solution)/shard_map/ppermute | solution.py:25
  162.3 169.3 %collective-permute-done.3 = bf16[8,512,512]{2,1,0:T(8,128)(2,1)} collective-permute-done((bf16[8,512,512]{2,1,0:T(8,128)(2,1)}, bf16[8,512,512]{2,1,0:T(8,128)(2,1)}, u32[]{:S(2)}, u32[]{:S(2)}) %collective-permute-start.3) | collective-permute-done | bytes 4194336 | tf_op jit(solution)/shard_map/ppermute | solution.py:25
  331.7 7.5 pad_maximum_fusion
  339.2 11.8 reverse_select_fusion
  386.2 22.9 %fusion.2 = (f32[8,512]{1,0:T(8,128)S(1)}, f32[8,512,3072]{2,1,0:T(8,128)}) fusion(pred[512,3072]{1,0:T(8,128)(4,1)} %broadcast_dynamic-update-slice_fusion, bf16[3072,8,64]{0,2,1:T(8,128)(2,1)} %bitcast.17, bf16[512,8,32]{0,2,1:T(8,128)(2,1)S(1)} %get-tuple-element.117, bf16[512,8,32]{0,2,1:T(8,128)(2,1)S(1)} %get-tuple-element.116), kind=kOutput, calls=%fused_computation.7 | convolution fusion | flops 1649405952 | bytes 55590912 | tf_op jit(solution)/shard_map/while/body/eval_jaxpr/qhd,khd->hqk/dot_general | solution.py:184
  409.1 23.0 %fusion = f32[8,512]{1,0:T(8,128)S(1)} fusion(f32[8,512,3072]{2,1,0:T(8,128)} %get-tuple-element.129, f32[8,512]{1,0:T(8,128)S(1)} %get-tuple-element.128, pred[512,3072]{1,0:T(8,128)(4,1)} %broadcast_dynamic-update-slice_fusion), kind=kLoop, calls=%fused_computation.5 | loop fusion | flops 62910464 | bytes 51937280 | tf_op jit(solution)/shard_map/while/body/eval_jaxpr/reduce_sum | solution.py:190
  432.2 22.6 %fusion.70 = (bf16[512,8,64]{0,2,1:T(8,128)(2,1)S(1)}, f32[512,8,64]{0,2,1:T(8,128)}) fusion(bf16[3072,8,64]{0,2,1:T(8,128)(2,1)} %bitcast.13, f32[8,512,3072]{2,1,0:T(8,128)} %get-tuple-element.129, f32[8,512]{1,0:T(8,128)S(1)} %fusion, f32[8,512]{1,0:T(8,128)S(1)} %get-tuple-element.128, pred[512,3072]{1,0:T(8,128)(4,1)} %broadcast_dynamic-update-slice_fusion), kind=kOutput, calls=%fused_computation.174 | convolution fusion | flops 1686372352 | bytes 56655872 | tf_op jit(solution)/shard_map/while/body/eval_jaxpr/hqk,khd->qhd/dot_general | solution.py:192
  457.6 40.1 %all-reduce.8.cloned.1.call-done = bf16[512,1024]{1,0:T(8,128)(2,1)} async-done(((bf16[512,1024]{1,0:T(8,128)(2,1)}), bf16[512,1024]{1,0:T(8,128)(2,1)}) %all-reduce.8.cloned.1.call-update) | async-done | bytes 1048592 | tf_op jit(solution)/shard_map/psum | solution.py:203
  514.5 40.1 %all-reduce.10.cloned.1.call-done = bf16[512,1024]{1,0:T(8,128)(2,1)} async-done(((bf16[512,1024]{1,0:T(8,128)(2,1)}), bf16[512,1024]{1,0:T(8,128)(2,1)}) %all-reduce.10.cloned.1.call-update) | async-done | bytes 1048592 | tf_op jit(solution)/shard_map/psum | solution.py:231
  562.1 24.3 %fusion.7 = f32[3072,8,64]{0,2,1:T(8,128)} fusion(bf16[512,8,64]{0,2,1:T(8,128)(2,1)} %bitcast.114, f32[8,512,3072]{2,1,0:T(8,128)} %get-tuple-element.129, f32[8,512]{1,0:T(8,128)S(1)} %log_add_fusion, pred[512,3072]{1,0:T(8,128)(4,1)} %broadcast_dynamic-update-slice_fusion), kind=kOutput, calls=%fused_computation.15 | convolution fusion | flops 1673527296 | bytes 58736640 | tf_op jit(solution)/shard_map/while/body/eval_jaxpr/hqk,qhd->khd/dot_general | solution.py:277
  586.4 33.0 %multiply_convert_fusion = bf16[8,512,3072]{2,1,0:T(8,128)(2,1)} fusion(f32[8,512,3072]{2,1,0:T(8,128)} %get-tuple-element.129, bf16[512,8,64]{0,2,1:T(8,128)(2,1)} %bitcast.115, bf16[3072,8,64]{0,2,1:T(8,128)(2,1)} %bitcast.13, f32[8,512]{1,0:T(8,128)S(1)} %bitcast.116, f32[8,512]{1,0:T(8,128)S(1)} %log_add_fusion, ...), kind=kOutput, calls=%fused_computation | convolution fusion | flops 1698693120 | bytes 80773120 | tf_op jit(solution)/shard_map/while/body/eval_jaxpr/qhd,khd->hqk/dot_general | solution.py:255
  619.4 10.7 multiply_bitcast_fusion
  645.5 5.6 fusion.68
  670.4 7.9 broadcast_in_dim.190.clone
  699.3 11.2 convert_element_type.206
  714.8 14.7 %fusion.31 = f32[512,8,64]{0,2,1:T(8,128)} fusion(bf16[3072,8,64]{0,2,1:T(8,128)(2,1)} %bitcast.17, bf16[8,512,3072]{2,1,0:T(8,128)(2,1)} %multiply_convert_fusion), kind=kOutput, calls=%fused_computation.69 | convolution fusion | flops 1610874880 | bytes 29360128 | tf_op jit(solution)/shard_map/while/body/eval_jaxpr/hqk,khd->qhd/dot_general | solution.py:260
  729.5 69.2 %reduce-scatter.3.cloned.1.call-done = bf16[512,512]{1,0:T(8,128)(2,1)} async-done(((bf16[8192,512]{1,0:T(8,128)(2,1)}), bf16[512,512]{1,0:T(8,128)(2,1)}) %reduce-scatter.3.cloned.1.call-update) | async-done | bytes 524304 | tf_op jit(solution)/shard_map/reduce_scatter | solution.py:306
  807.1 99.8 %reduce-scatter.5.cloned.1.call-done = bf16[512,512]{1,0:T(8,128)(2,1)} async-done(((bf16[8192,512]{1,0:T(8,128)(2,1)}), bf16[512,512]{1,0:T(8,128)(2,1)}) %reduce-scatter.5.cloned.1.call-update) | async-done | bytes 524304 | tf_op jit(solution)/shard_map/reduce_scatter | solution.py:309
  913.5 5.2 convolution_convert_fusion.1
  933.5 42.9 %all-reduce.14.cloned.1.call-done = (bf16[512,1024]{1,0:T(8,128)(2,1)}, bf16[512,1024]{1,0:T(8,128)(2,1)}) async-done(((bf16[512,1024]{1,0:T(8,128)(2,1)}, bf16[512,1024]{1,0:T(8,128)(2,1)}), (bf16[512,1024]{1,0:T(8,128)(2,1)}, bf16[512,1024]{1,0:T(8,128)(2,1)})) %all-reduce.14.cloned.1.call-update) | async-done | bytes 2097168 | tf_op jit(solution)/shard_map/psum | solution.py:214
  978.9 34.7 %all-reduce = (bf16[1024]{0:T(1024)(128)(2,1)S(1)}, bf16[1024]{0:T(1024)(128)(2,1)S(1)}) all-reduce(bf16[1024]{0:T(1024)(128)(2,1)S(1)} %get-tuple-element.62, bf16[1024]{0:T(1024)(128)(2,1)S(1)} %copy-done.57), channel_id=1, replica_groups=mesh['dp'=16,'tensor'=2] {'dp'}, use_global_device_ids=true, to_apply=%region_29.30 | all-reduce | flops 2048 | bytes 8192 | tf_op jit(solution)/shard_map/psum | solution.py:345
  1014.7 4.9 fusion.19
  1019.7 207.5 %all-reduce.12.cloned.1.call-done = (bf16[1024,512]{1,0:T(8,128)(2,1)}, bf16[1024,512]{1,0:T(8,128)(2,1)}, bf16[1024,512]{1,0:T(8,128)(2,1)}, bf16[512,1024]{1,0...) async-done(((bf16[1024,512]{1,0:T(8,128)(2,1)}, bf16[1024,512]{1,0:T(8,128)(2,1)}, bf16[1024,512]{1,0:T(8,128)(2,1)}, ...) | async-done | bytes 12845072 | tf_op jit(solution)/shard_map/psum | solution.py:338
  (279 shorter events, 216.9 us)
Async XLA Ops:
  7.2 498.6 %copy-start = (bf16[1408,1024]{1,0:T(8,128)(2,1)S(1)}, bf16[1408,1024]{1,0:T(8,128)(2,1)}, u32[]{:S(2)}) copy-start(bf16[1408,1024]{1,0:T(8,128)(2,1)} %param.23) | copy-start | bytes 8650756
  7.2 367.8 %all-gather.2.cloned.1.call-start = ((), (), s32[]{:S(2)}) async-start(), calls=%async_computation.2 | async-start | bytes 8912896 | tf_op jit(solution)/shard_map/all_gather | solution.py:173
  8.9 9.8 copy-start.53
  9.7 9.1 copy-start.49
  17.2 368.9 %copy-start.23 = (bf16[512,8,32]{0,2,1:T(8,128)(2,1)}, bf16[512,8,32]{0,2,1:T(8,128)(2,1)S(1)}, u32[]{:S(2)}) copy-start(bf16[512,8,32]{0,2,1:T(8,128)(2,1)S(1)} %get-tuple-element.116) | copy-start | bytes 786436
  17.3 368.9 %copy-start.25 = (bf16[512,8,32]{0,2,1:T(8,128)(2,1)}, bf16[512,8,32]{0,2,1:T(8,128)(2,1)S(1)}, u32[]{:S(2)}) copy-start(bf16[512,8,32]{0,2,1:T(8,128)(2,1)S(1)} %get-tuple-element.117) | copy-start | bytes 786436
  18.2 479.5 %all-reduce.8.cloned.1.call-start = ((), (), s32[]{:S(2)}) async-start(), calls=%async_computation.3 | async-start | bytes 2097152 | tf_op jit(solution)/shard_map/psum | solution.py:203
  22.0 2.3 collective-permute-start
  27.2 32.3 %collective-permute-start.1 = (bf16[2,512,512]{2,1,0:T(8,128)(2,1)}, bf16[2,512,512]{2,1,0:T(8,128)(2,1)}, u32[]{:S(2)}, u32[]{:S(2)}) collective-permute-start(bf16[2,512,512]{2,1,0:T(8,128)(2,1)} %get-tuple-element.121), channel_id=1, source_target_pairs={{0,4},{2,6},{4,0},{6,2},{8,12},{10,14},{12,8},{14,10},{16,20},{18,... | collective-permute-start | bytes 3145736 | tf_op jit(solution)/shard_map/ppermute | solution.py:25
  63.0 79.9 %collective-permute-start.2 = (bf16[4,512,512]{2,1,0:T(8,128)(2,1)}, bf16[4,512,512]{2,1,0:T(8,128)(2,1)}, u32[]{:S(2)}, u32[]{:S(2)}) collective-permute-start(bf16[4,512,512]{2,1,0:T(8,128)(2,1)} %bitcast.7), channel_id=1, source_target_pairs={{0,8},{2,10},{4,12},{6,14},{8,0},{10,2},{12,4},{14,6},{16,24},{18,... | collective-permute-start | bytes 6291464 | tf_op jit(solution)/shard_map/ppermute | solution.py:25
  148.4 183.2 %collective-permute-start.3 = (bf16[8,512,512]{2,1,0:T(8,128)(2,1)}, bf16[8,512,512]{2,1,0:T(8,128)(2,1)}, u32[]{:S(2)}, u32[]{:S(2)}) collective-permute-start(bf16[8,512,512]{2,1,0:T(8,128)(2,1)} %bitcast.10), channel_id=1, source_target_pairs={{0,16},{2,18},{4,20},{6,22},{8,24},{10,26},{12,28},{14,30},{16,0},... | collective-permute-start | bytes 12582920 | tf_op jit(solution)/shard_map/ppermute | solution.py:25
  432.1 23.4 %copy-start.62 = (bf16[512,1024]{1,0:T(8,128)(2,1)S(1)}, bf16[512,1024]{1,0:T(8,128)(2,1)}, u32[]{:S(2)}) copy-start(bf16[512,1024]{1,0:T(8,128)(2,1)} %param.20) | copy-start | bytes 3145732
  457.3 97.3 %all-reduce.10.cloned.1.call-start = ((), (), s32[]{:S(2)}) async-start(), calls=%async_computation.4 | async-start | bytes 2097152 | tf_op jit(solution)/shard_map/psum | solution.py:231
  457.6 100.5 %copy-start.47 = (f32[1024]{0:T(1024)}, f32[1024]{0:T(1024)S(1)}, u32[]{:S(2)}) copy-start(f32[1024]{0:T(1024)S(1)} %convert_element_type.187) | copy-start | bytes 12292
  499.8 58.3 %copy-start.51 = (f32[512]{0:T(512)}, f32[512]{0:T(512)S(1)}, u32[]{:S(2)}) copy-start(f32[512]{0:T(512)S(1)} %add_rsqrt_fusion) | copy-start | bytes 6148
  514.4 284.3 %reduce-scatter.3.cloned.1.call-start = ((), (), s32[]{:S(2)}) async-start(), calls=%async_computation.5 | async-start | bytes 8912896 | tf_op jit(solution)/shard_map/reduce_scatter | solution.py:306
  586.4 33.0 %copy-start.24 = (bf16[512,8,32]{0,2,1:T(8,128)(2,1)S(1)}, bf16[512,8,32]{0,2,1:T(8,128)(2,1)}, u32[]{:S(2)}) copy-start(bf16[512,8,32]{0,2,1:T(8,128)(2,1)} %copy-done.23) | copy-start | bytes 786436
  586.4 33.0 %copy-start.26 = (bf16[512,8,32]{0,2,1:T(8,128)(2,1)S(1)}, bf16[512,8,32]{0,2,1:T(8,128)(2,1)}, u32[]{:S(2)}) copy-start(bf16[512,8,32]{0,2,1:T(8,128)(2,1)} %copy-done.25) | copy-start | bytes 786436
  693.9 213.0 %reduce-scatter.5.cloned.1.call-start = ((), (), s32[]{:S(2)}) async-start(), calls=%async_computation.6 | async-start | bytes 8912896 | tf_op jit(solution)/shard_map/reduce_scatter | solution.py:309
  710.5 266.0 %all-reduce.14.cloned.1.call-start = ((), (), s32[]{:S(2)}) async-start(), calls=%async_computation.8 | async-start | bytes 4194304 | tf_op jit(solution)/shard_map/psum | solution.py:214
  714.8 86.1 %copy-start.44 = (f32[512,32]{0,1:T(8,128)S(1)}, f32[512,32]{0,1:T(8,128)}, u32[]{:S(2)}) copy-start(f32[512,32]{0,1:T(8,128)} %copy-done.43) | copy-start | bytes 196612
  714.8 86.1 %copy-start.46 = (f32[512,32]{0,1:T(8,128)S(1)}, f32[512,32]{0,1:T(8,128)}, u32[]{:S(2)}) copy-start(f32[512,32]{0,1:T(8,128)} %copy-done.45) | copy-start | bytes 196612
  913.4 313.7 %all-reduce.12.cloned.1.call-start = ((), (), s32[]{:S(2)}) async-start(), calls=%async_computation.7 | async-start | bytes 25690112 | tf_op jit(solution)/shard_map/psum | solution.py:338
  933.5 45.3 %copy-start.57 = (bf16[1024]{0:T(1024)(128)(2,1)S(1)}, bf16[1024]{0:T(1024)(128)(2,1)}, u32[]{:S(2)}) copy-start(bf16[1024]{0:T(1024)(128)(2,1)} %get-tuple-element.60) | copy-start | bytes 6148
  (58 other events, 207.6 us)
Sparse Core Ops, SparseCore 0:
  18.3 108.2 all-gather.1
  457.4 40.1 all-reduce.7
  514.5 40.0 all-reduce.9
  694.1 104.5 reduce-scatter.2
  802.6 104.3 reduce-scatter.4
  913.6 62.8 all-reduce.13
  984.1 243.0 all-reduce.11
